TPU v7x, 32 devices: a whole 2x2x4 slice. The times are simulated.
32 devices in a mesh: groups: 2 (over y), st: 4 (over x, core), ch: 4 (over z).
Axes of the slice: x: 2, y: 2, z: 4, core: 2. Of those that a mesh axis runs over, the one named last changes fastest.
Arguments:
- latents: bfloat16 [1280, 1024], P('ch', ('groups', 'st')), parts along dimension 1, may hold values from -6 to 6
- spatial_weight: bfloat16 [9, 1280, 1280], P(None, 'ch'), may hold values from -0.0546875 to 0.0546875
- temporal_weight: bfloat16 [3, 1280, 1280], P(None, 'ch'), may hold values from -0.09375 to 0.09375
- cotangent: bfloat16 [1280, 1024], P('ch', ('groups', 'st')), parts along dimension 1, may hold values from -6 to 6
Outputs:
- temporal_out: bfloat16 [1280, 1024], P('ch', ('groups', 'st')), parts along dimension 1
- latent_grad: bfloat16 [1280, 1024], P('ch', ('groups', 'st')), parts along dimension 1
- spatial_grad: float32 [18, 1280, 1280], P('groups', 'ch', 'st'), parts along dimension 0
- temporal_grad: float32 [6, 1280, 1280], P('groups', 'ch', 'st'), parts along dimension 0
There are 2 independent parts, one for each index of `groups`. A program takes and returns all parts, laid end to end along the dimension named above; an argument that names none is the same for every part. Nothing has to cross between parts.
All inputs are finite; a program needn't handle non-finite values.
Results may differ from a plain program's by a relative error of at most 0.008.
Values may be sent and summed in bfloat16 or wider, within the bound.
No kernel may reach another device: no remote copies, remote signals or barrier semaphores. Data moves between devices by JAX's collectives and lax.ppermute only.
A program may use at most 192 MiB of HBM per device.

v0:
```python
import math
import jax
import jax.numpy as jnp
from jax import lax
from jax.sharding import PartitionSpec as P

FT = 2
RT = 2
W = 32
RBANDS = 2
spatial_offsets = tuple(
    ((row_step, col_step) for row_step in (-1, 0, 1) for col_step in (-1, 0, 1))
)
frame_offsets = (-1, 0, 1)


def passed_along(shard, axis, by):
    devices = lax.axis_size(axis)
    pairs = [(i, i + by) for i in range(devices) if 0 <= i + by < devices]
    return lax.ppermute(shard, axis, pairs)


def neighbour(slab, distance):
    return passed_along(slab, "st", distance)


def circulate(data, fold, initial):
    return fold(initial, lax.all_gather(data, "ch", axis=0, tiled=True), jnp.int32(0))


def regather(data, build):
    return build(lax.all_gather(data, "ch", axis=0, tiled=True), jnp.int32(0))


def pad_rows(field):
    channels = field.shape[0]
    layered = field.reshape(channels, FT, RT * W)
    band = lax.axis_index("st") % RBANDS
    upper = neighbour(layered[:, :, (RT - 1) * W :], 1)
    lower = neighbour(layered[:, :, :W], -1)
    upper = jnp.where(band > 0, upper, jnp.zeros_like(upper))
    lower = jnp.where(band < RBANDS - 1, lower, jnp.zeros_like(lower))
    margin = jnp.zeros((channels, FT, 1), field.dtype)
    return jnp.concatenate([margin, upper, layered, lower, margin], axis=2)


def spatial_piece(padded, row_step, col_step):
    first_cell = 1 + (1 + row_step) * W + col_step
    window = lax.slice_in_dim(padded, first_cell, first_cell + RT * W, axis=2)
    column = jnp.arange(RT * W, dtype=jnp.int32) % W + col_step
    inside = (column >= 0) & (column < W)
    window = jnp.where(inside, window, jnp.zeros_like(window))
    return window.reshape(padded.shape[0], FT * RT * W)


def pad_frames(field):
    frame_cells = RT * W
    earlier = neighbour(field[:, (FT - 1) * frame_cells :], RBANDS)
    following = neighbour(field[:, :frame_cells], -RBANDS)
    return jnp.concatenate([earlier, field, following], axis=1)


def frame_piece(padded, frame_step):
    frame_cells = RT * W
    first_cell = (1 + frame_step) * frame_cells
    return lax.slice_in_dim(padded, first_cell, first_cell + FT * frame_cells, axis=1)


def contract(weights, pieces):
    running = jnp.dot(weights[0], pieces[0], preferred_element_type=jnp.float32)
    for position in range(1, len(pieces)):
        running = running + jnp.dot(
            weights[position], pieces[position], preferred_element_type=jnp.float32
        )
    return running


def outer_sums(gradient, pieces):
    contraction = (((1,), (1,)), ((), ()))
    return jnp.stack(
        [
            lax.dot_general(gradient, tap_piece, contraction, preferred_element_type=jnp.float32)
            for tap_piece in pieces
        ]
    )


def on_device(latents, spatial_weight, temporal_weight, cotangent):
    channels, tile_cells = latents.shape
    grad_scale = 1.0 / math.sqrt(tile_cells * lax.axis_size("st"))
    spatial_back, temporal_back = (
        lax.all_to_all(
            jnp.transpose(spatial_weight, (0, 2, 1)), "ch", split_axis=1, concat_axis=2, tiled=True
        ),
        lax.all_to_all(
            jnp.transpose(temporal_weight, (0, 2, 1)), "ch", split_axis=1, concat_axis=2, tiled=True
        ),
    )
    empty_sum = jnp.zeros((channels, tile_cells), jnp.float32)
    latent_pad = pad_rows(latents)
    latent_store = jnp.zeros((1,), jnp.bfloat16)

    def spatial_forward(carry, portion, offset):
        running, stored = carry
        running = contract(
            spatial_weight,
            [spatial_piece(portion, row_step, col_step) for row_step, col_step in spatial_offsets],
        )
        return (running, stored)

    spatial_sum, latent_store = circulate(latent_pad, spatial_forward, (empty_sum, latent_store))
    hidden = (latents.astype(jnp.float32) + spatial_sum).astype(jnp.bfloat16)
    hidden_pad = pad_frames(hidden)
    hidden_store = jnp.zeros((1,), jnp.bfloat16)

    def temporal_forward(carry, portion, offset):
        running, stored = carry
        running = contract(
            temporal_weight, [frame_piece(portion, frame_step) for frame_step in frame_offsets]
        )
        return (running, stored)

    temporal_sum, hidden_store = circulate(hidden_pad, temporal_forward, (empty_sum, hidden_store))
    temporal_out = (hidden.astype(jnp.float32) + temporal_sum).astype(jnp.bfloat16)
    upstream_pad = pad_frames(cotangent)

    def temporal_backward(running, portion, offset):
        return contract(
            temporal_back, [frame_piece(portion, -frame_step) for frame_step in frame_offsets]
        )

    hidden_back = circulate(upstream_pad, temporal_backward, empty_sum)

    def temporal_terms(portion, offset):
        return outer_sums(
            cotangent, [frame_piece(portion, frame_step) for frame_step in frame_offsets]
        )

    temporal_grads = regather(hidden_pad, temporal_terms)
    hidden_grad = (cotangent.astype(jnp.float32) + hidden_back).astype(jnp.bfloat16)
    grad_pad = pad_rows(hidden_grad)

    def spatial_backward(running, portion, offset):
        return contract(
            spatial_back,
            [
                spatial_piece(portion, -row_step, -col_step)
                for row_step, col_step in spatial_offsets
            ],
        )

    latent_back = circulate(grad_pad, spatial_backward, empty_sum)

    def spatial_terms(portion, offset):
        return outer_sums(
            hidden_grad,
            [spatial_piece(portion, row_step, col_step) for row_step, col_step in spatial_offsets],
        )

    spatial_grads = regather(latent_pad, spatial_terms)
    latent_grad = (hidden_grad.astype(jnp.float32) + latent_back).astype(jnp.bfloat16)
    spatial_total, temporal_total = (
        lax.psum_scatter(
            spatial_grads.astype(jnp.bfloat16), "st", scatter_dimension=2, tiled=True
        ).astype(jnp.float32),
        lax.psum_scatter(
            temporal_grads.astype(jnp.bfloat16), "st", scatter_dimension=2, tiled=True
        ).astype(jnp.float32),
    )
    return (temporal_out, latent_grad, spatial_total * grad_scale, temporal_total * grad_scale)


def solution(mesh):
    return jax.shard_map(
        on_device,
        mesh=mesh,
        in_specs=(
            P("ch", ("groups", "st")),
            P(None, "ch", None),
            P(None, "ch", None),
            P("ch", ("groups", "st")),
        ),
        out_specs=(
            P("ch", ("groups", "st")),
            P("ch", ("groups", "st")),
            P("groups", "ch", "st"),
            P("groups", "ch", "st"),
        ),
        check_vma=False,
    )
```

profile of v0, /device:TPU:0, one launch (start us, length us, event | category | flops | bytes accessed | tf_op | source)
XLA Modules:
  0.0 648.7 jit_solution(954349262117856633)
XLA Ops:
  7.2 7.7 %copy.23 = bf16[3,320,1280]{1,0,2:T(4,128)(2,1)} copy(bf16[3,320,1280]{2,1,0:T(8,128)(2,1)} %param.6) | data formatting | bytes 4915200 | tf_op args[2]
  14.9 6.3 all-to-all-start
  22.6 4.6 collective-permute-start.4
  33.0 87.4 %all_gather.16 = bf16[1280,256]{1,0:T(8,128)(2,1)S(1)} all-gather(bf16[320,256]{1,0:T(8,128)(2,1)S(1)} %pad_maximum_fusion.2), channel_id=1, replica_groups=mesh['groups'=2,'st'=4,'ch'=4] {'ch'}, dimensions={0}, use_global_device_ids=true | all-gather | bytes 819200 | tf_op jit(solution)/shard_map/all_gather | solution.py:28
  120.4 24.1 %all_gather.14 = bf16[1280,2,130]{2,1,0:T(2,128)(2,1)S(1)} all-gather(bf16[320,2,130]{2,1,0:T(2,128)(2,1)S(1)} %copy.13), channel_id=1, replica_groups=mesh['groups'=2,'st'=4,'ch'=4] {'ch'}, dimensions={0}, use_global_device_ids=true | all-gather | bytes 832000 | tf_op jit(solution)/shard_map/all_gather | solution.py:28
  144.4 4.9 copy.63
  149.3 2.3 fusion.70
  151.6 2.8 squeeze.85
  154.4 2.8 squeeze.84
  165.1 6.9 %fusion.72 = (bf16[1280,2,64]{2,1,0:T(2,128)(2,1)S(1)}, bf16[1280,2,64]{2,1,0:T(2,128)(2,1)}, bf16[1280,2,64]{2,1,0:T(2,128)(2,1)}, bf16[1280,2,64]{2,1,0:T(2,12...) fusion(bf16[1280,2,130]{2,1,0:T(2,128)(2,1)S(1)} %all_gather.14), kind=kLoop, calls=%fused_computation.137 | loop fusion | bytes 5898240 | tf_op jit(solution)/shard_map/slice | solution.py:49
  172.1 2.0 copy.45
  174.1 2.0 copy.48
  176.1 2.0 copy.42
  178.1 2.0 copy.46
  180.1 2.0 copy.49
  182.2 2.0 copy.43
  189.7 3.7 collective-permute-done.7
  194.4 24.4 %all_gather.17 = bf16[1280,2,130]{2,1,0:T(2,128)(2,1)S(1)} all-gather(bf16[320,2,130]{2,1,0:T(2,128)(2,1)S(1)} %copy.26), channel_id=1, replica_groups=mesh['groups'=2,'st'=4,'ch'=4] {'ch'}, dimensions={0}, use_global_device_ids=true | all-gather | bytes 832000 | tf_op jit(solution)/shard_map/all_gather | solution.py:28
  218.8 6.9 %fusion.71 = (bf16[1280,2,64]{2,1,0:T(2,128)(2,1)S(1)}, bf16[1280,2,64]{2,1,0:T(2,128)(2,1)}, bf16[1280,2,64]{2,1,0:T(2,128)(2,1)}, bf16[1280,2,64]{2,1,0:T(2,12...) fusion(bf16[1280,2,130]{2,1,0:T(2,128)(2,1)S(1)} %all_gather.17), kind=kLoop, calls=%fused_computation.136 | loop fusion | bytes 5898240 | tf_op jit(solution)/shard_map/slice | solution.py:49
  229.0 2.2 copy.58
  233.2 2.0 copy.55
  239.2 2.0 copy.54
  241.3 2.7 broadcast_select_fusion.12
  246.2 2.5 broadcast_select_fusion.6
  254.5 4.6 collective-permute-start.2
  261.2 17.7 %all_gather.15 = bf16[1280,256]{1,0:T(8,128)(2,1)S(1)} all-gather(bf16[320,256]{1,0:T(8,128)(2,1)S(1)} %pad_maximum_fusion.1), channel_id=1, replica_groups=mesh['groups'=2,'st'=4,'ch'=4] {'ch'}, dimensions={0}, use_global_device_ids=true | all-gather | bytes 819200 | tf_op jit(solution)/shard_map/all_gather | solution.py:28
  280.4 6.0 copy.40
  286.5 8.3 %reshape.123 = bf16[1280,960]{1,0:T(8,128)(2,1)} reshape(bf16[1280,3,320]{2,1,0:T(4,128)(2,1)} %bitcast.203) | data formatting | bytes 4915200
  294.9 20.9 %copy.28 = bf16[9,320,1280]{1,0,2:T(8,128)(2,1)} copy(bf16[9,320,1280]{2,1,0:T(8,128)(2,1)} %param.5) | data formatting | bytes 14745600 | tf_op args[1]
  327.3 20.2 %copy.38 = bf16[9,320,1280]{1,0,2:T(8,128)(2,1)} copy(bf16[9,320,1280]{2,1,0:T(8,128)(2,1)} %fusion.17) | data formatting | bytes 14745600
  347.5 18.7 %reshape.121 = bf16[1280,2880]{1,0:T(8,128)(2,1)} reshape(bf16[1280,9,320]{2,1,0:T(8,128)(2,1)} %bitcast.197) | data formatting | bytes 14745600
  366.3 14.2 %bitcast_bitcast_fusion = bf16[1280,9,320]{2,1,0:T(8,128)(2,1)} fusion(bf16[9,320,1280]{1,0,2:T(8,128)(2,1)} %copy.28), kind=kLoop, calls=%fused_computation.142 | loop fusion | bytes 14745600
  380.5 15.3 %reshape.125 = bf16[4,2,460800]{2,1,0:T(2,128)(2,1)} reshape(bf16[1280,9,320]{2,1,0:T(8,128)(2,1)} %bitcast_bitcast_fusion) | data formatting | bytes 14745600
  395.8 6.0 all-to-all-start.1
  403.7 2.5 reshape.124
  408.6 152.6 %all-to-all-done.1 = bf16[4,2,460800]{2,1,0:T(2,128)(2,1)} async-done(((bf16[4,2,460800]{2,1,0:T(2,128)(2,1)}), bf16[4,2,460800]{2,1,0:T(2,128)(2,1)}, u32[]{:S(2)}, u32[]{:S(2)}) %all-to-all-start.1) | async-done | bytes 7372832 | tf_op jit(solution)/shard_map/all_to_all | solution.py:92
  561.2 16.0 %reshape.126 = bf16[1280,9,320]{2,1,0:T(8,128)(2,1)} reshape(bf16[4,2,460800]{2,1,0:T(2,128)(2,1)} %all-to-all-done.1) | data formatting | bytes 14745600
  577.1 12.7 %copy.62 = bf16[9,4,320,320]{3,1,2,0:T(4,128)(2,1)S(1)} copy(bf16[9,4,320,320]{3,0,2,1:T(8,128)(2,1)} %bitcast.198) | data formatting | bytes 14745600 | tf_op jit(solution)/shard_map/all_to_all | solution.py:92
  589.9 4.4 fusion.69
  594.3 2.8 squeeze.87
  597.0 2.8 squeeze.88
  599.8 2.8 squeeze.89
  602.6 2.9 squeeze.90
  605.5 2.8 squeeze.91
  608.2 2.8 squeeze.92
  627.6 5.6 reshape.122
  633.2 6.0 copy.39
  639.2 2.5 convert_multiply_fusion
  (158 shorter events, 74.8 us)
Async XLA Ops:
  7.2 14.0 %copy-start = (bf16[320,128]{1,0:T(8,128)(2,1)S(1)}, bf16[320,128]{1,0:T(8,128)(2,1)}, u32[]{:S(2)}) copy-start(bf16[320,128]{1,0:T(8,128)(2,1)} %param.7) | copy-start | bytes 245764
  7.2 20.0 %copy-start.29 = (bf16[320,128]{1,0:T(8,128)(2,1)S(1)}, bf16[320,128]{1,0:T(8,128)(2,1)}, u32[]{:S(2)}) copy-start(bf16[320,128]{1,0:T(8,128)(2,1)} %param.4) | copy-start | bytes 245764
  14.9 129.6 %all-to-all-start = ((bf16[3,1280,320]{2,0,1:T(4,128)(2,1)}), bf16[3,1280,320]{2,0,1:T(4,128)(2,1)}, u32[]{:S(2)}, u32[]{:S(2)}) async-start(bf16[3,1280,320]{2,0,1:T(4,128)(2,1)} %bitcast.202), calls=%async_computation | async-start | bytes 7864320 | tf_op jit(solution)/shard_map/all_to_all | solution.py:95
  21.2 382.5 %reduce-scatter.9.cloned.1.call-start = ((), (), s32[]{:S(2)}) async-start(), calls=%async_computation.5 | async-start | bytes 3276800
  21.3 11.5 %collective-permute-start.5 = (bf16[320,64]{1,0:T(8,128)(2,1)S(1)}, bf16[320,64]{1,0:T(8,128)(2,1)S(1)}, u32[]{:S(2)}, u32[]{:S(2)}) collective-permute-start(bf16[320,64]{1,0:T(8,128)(2,1)S(1)} %get-tuple-element.39), channel_id=1, source_target_pairs={{8,0},{12,4},{9,1},{13,5},{10,2},{14,6},{11,3},{15,7},{24,16},{28,... | collective-permute-start | bytes 122888 | tf_op jit(solution)/shard_map/ppermute | solution.py:20
  22.6 10.2 %collective-permute-start.4 = (bf16[320,64]{1,0:T(8,128)(2,1)S(1)}, bf16[320,64]{1,0:T(8,128)(2,1)S(1)}, u32[]{:S(2)}, u32[]{:S(2)}) collective-permute-start(bf16[320,64]{1,0:T(8,128)(2,1)S(1)} %get-tuple-element.38), channel_id=1, source_target_pairs={{0,8},{4,12},{1,9},{5,13},{2,10},{6,14},{3,11},{7,15},{16,24},{20,... | collective-permute-start | bytes 122888 | tf_op jit(solution)/shard_map/ppermute | solution.py:20
  27.3 2.7 collective-permute-start
  28.6 3.1 collective-permute-start.1
  163.6 26.1 %collective-permute-start.6 = (bf16[320,2,32]{0,2,1:T(8,128)(2,1)S(1)}, bf16[320,2,32]{0,2,1:T(8,128)(2,1)S(1)}, u32[]{:S(2)}, u32[]{:S(2)}) collective-permute-start(bf16[320,2,32]{0,2,1:T(8,128)(2,1)S(1)} %get-tuple-element.35), channel_id=1, source_target_pairs={{0,4},{4,8},{8,12},{1,5},{5,9},{9,13},{2,6},{6,10},{10,14},{3,7},{... | collective-permute-start | bytes 122888 | tf_op jit(solution)/shard_map/ppermute | solution.py:20
  188.4 5.0 collective-permute-start.7
  229.0 19.7 %slice-start = ((s8[7372800]{0:T(1024)(128)(4,1)}), s8[3178496]{0:T(1024)(128)(4,1)S(1)}, s32[]{:S(2)}) async-start(s8[7372800]{0:T(1024)(128)(4,1)} %bitcast.200), calls=%async_computation.6 | async-start | bytes 6356992
  241.3 7.5 %slice-start.1 = ((s8[7372800]{0:T(1024)(128)(4,1)}), s8[4194304]{0:T(1024)(128)(4,1)S(1)}, s32[]{:S(2)}) async-start(s8[7372800]{0:T(1024)(128)(4,1)} %bitcast.200), calls=%async_computation.7 | async-start | bytes 8388608
  241.3 7.9 %copy-start.21 = (bf16[1280,2,64]{0,2,1:T(8,128)(2,1)S(1)}, bf16[1280,2,64]{0,2,1:T(8,128)(2,1)}, u32[]{:S(2)}) copy-start(bf16[1280,2,64]{0,2,1:T(8,128)(2,1)} %copy.47) | copy-start | bytes 983044
  241.3 7.9 %copy-start.22 = (bf16[1280,2,64]{0,2,1:T(8,128)(2,1)S(1)}, bf16[1280,2,64]{0,2,1:T(8,128)(2,1)}, u32[]{:S(2)}) copy-start(bf16[1280,2,64]{0,2,1:T(8,128)(2,1)} %copy.50) | copy-start | bytes 983044
  241.3 7.9 %copy-start.23 = (bf16[1280,2,64]{0,2,1:T(8,128)(2,1)S(1)}, bf16[1280,2,64]{0,2,1:T(8,128)(2,1)}, u32[]{:S(2)}) copy-start(bf16[1280,2,64]{0,2,1:T(8,128)(2,1)} %copy.44) | copy-start | bytes 983044
  241.3 7.9 %copy-start.26 = (bf16[1280,2,64]{0,2,1:T(8,128)(2,1)S(1)}, bf16[1280,2,64]{0,2,1:T(8,128)(2,1)}, u32[]{:S(2)}) copy-start(bf16[1280,2,64]{0,2,1:T(8,128)(2,1)} %copy.57) | copy-start | bytes 983044
  241.3 7.9 %copy-start.27 = (bf16[1280,2,64]{0,2,1:T(8,128)(2,1)S(1)}, bf16[1280,2,64]{0,2,1:T(8,128)(2,1)}, u32[]{:S(2)}) copy-start(bf16[1280,2,64]{0,2,1:T(8,128)(2,1)} %copy.51) | copy-start | bytes 983044
  241.3 7.9 %copy-start.28 = (bf16[1280,2,64]{0,2,1:T(8,128)(2,1)S(1)}, bf16[1280,2,64]{0,2,1:T(8,128)(2,1)}, u32[]{:S(2)}) copy-start(bf16[1280,2,64]{0,2,1:T(8,128)(2,1)} %copy.54) | copy-start | bytes 983044
  244.0 0.7 copy-start.19
  244.0 7.5 %copy-start.5 = (bf16[1280,2,64]{0,2,1:T(8,128)(2,1)}, bf16[1280,2,64]{0,2,1:T(8,128)(2,1)S(1)}, u32[]{:S(2)}) copy-start(bf16[1280,2,64]{0,2,1:T(8,128)(2,1)S(1)} %get-tuple-element.43) | copy-start | bytes 983044
  244.0 7.9 %copy-start.3 = (bf16[1280,2,64]{0,2,1:T(8,128)(2,1)}, bf16[1280,2,64]{0,2,1:T(8,128)(2,1)S(1)}, u32[]{:S(2)}) copy-start(bf16[1280,2,64]{0,2,1:T(8,128)(2,1)S(1)} %get-tuple-element.44) | copy-start | bytes 983044
  248.7 4.3 copy-start.7
  248.8 4.3 copy-start.9
  248.8 4.3 copy-start.11
  250.3 29.4 %copy-start.13 = (bf16[1280,2,64]{0,2,1:T(8,128)(2,1)}, bf16[1280,2,64]{0,2,1:T(8,128)(2,1)S(1)}, u32[]{:S(2)}) copy-start(bf16[1280,2,64]{0,2,1:T(8,128)(2,1)S(1)} %get-tuple-element.55) | copy-start | bytes 983044
  250.3 29.4 %copy-start.15 = (bf16[1280,2,64]{0,2,1:T(8,128)(2,1)}, bf16[1280,2,64]{0,2,1:T(8,128)(2,1)S(1)}, u32[]{:S(2)}) copy-start(bf16[1280,2,64]{0,2,1:T(8,128)(2,1)S(1)} %get-tuple-element.59) | copy-start | bytes 983044
  250.3 29.5 %copy-start.24 = (bf16[1280,2,64]{0,2,1:T(8,128)(2,1)}, bf16[1280,2,64]{0,2,1:T(8,128)(2,1)S(1)}, u32[]{:S(2)}) copy-start(bf16[1280,2,64]{0,2,1:T(8,128)(2,1)S(1)} %get-tuple-element.56) | copy-start | bytes 983044
  253.2 6.3 collective-permute-start.3
  254.5 6.6 %collective-permute-start.2 = (bf16[320,64]{1,0:T(8,128)(2,1)S(1)}, bf16[320,64]{1,0:T(8,128)(2,1)S(1)}, u32[]{:S(2)}, u32[]{:S(2)}) collective-permute-start(bf16[320,64]{1,0:T(8,128)(2,1)S(1)} %get-tuple-element.40), channel_id=1, source_target_pairs={{0,8},{4,12},{1,9},{5,13},{2,10},{6,14},{3,11},{7,15},{16,24},{20,... | collective-permute-start | bytes 122888 | tf_op jit(solution)/shard_map/ppermute | solution.py:20
  294.8 21.0 %copy-start.20 = (bf16[1280,2,64]{0,2,1:T(8,128)(2,1)S(1)}, bf16[1280,2,64]{0,2,1:T(8,128)(2,1)}, u32[]{:S(2)}) copy-start(bf16[1280,2,64]{0,2,1:T(8,128)(2,1)} %copy-done.19) | copy-start | bytes 983044
  294.8 22.3 %copy-start.12 = (bf16[1280,2,64]{0,2,1:T(8,128)(2,1)S(1)}, bf16[1280,2,64]{0,2,1:T(8,128)(2,1)}, u32[]{:S(2)}) copy-start(bf16[1280,2,64]{0,2,1:T(8,128)(2,1)} %copy-done.11) | copy-start | bytes 983044
  294.8 23.6 %copy-start.16 = (bf16[1280,2,64]{0,2,1:T(8,128)(2,1)S(1)}, bf16[1280,2,64]{0,2,1:T(8,128)(2,1)}, u32[]{:S(2)}) copy-start(bf16[1280,2,64]{0,2,1:T(8,128)(2,1)} %copy-done.15) | copy-start | bytes 983044
  294.8 24.9 %copy-start.6 = (bf16[1280,2,64]{0,2,1:T(8,128)(2,1)S(1)}, bf16[1280,2,64]{0,2,1:T(8,128)(2,1)}, u32[]{:S(2)}) copy-start(bf16[1280,2,64]{0,2,1:T(8,128)(2,1)} %copy-done.5) | copy-start | bytes 983044
  294.8 26.1 %copy-start.10 = (bf16[1280,2,64]{0,2,1:T(8,128)(2,1)S(1)}, bf16[1280,2,64]{0,2,1:T(8,128)(2,1)}, u32[]{:S(2)}) copy-start(bf16[1280,2,64]{0,2,1:T(8,128)(2,1)} %copy-done.9) | copy-start | bytes 983044
  294.8 27.4 %copy-start.14 = (bf16[1280,2,64]{0,2,1:T(8,128)(2,1)S(1)}, bf16[1280,2,64]{0,2,1:T(8,128)(2,1)}, u32[]{:S(2)}) copy-start(bf16[1280,2,64]{0,2,1:T(8,128)(2,1)} %copy-done.13) | copy-start | bytes 983044
  294.8 332.8 %reduce-scatter.7.cloned.1.call-start = ((), (), s32[]{:S(2)}) async-start(), calls=%async_computation.4 | async-start | bytes 9420800
  315.8 7.7 %copy-start.4 = (bf16[1280,2,64]{0,2,1:T(8,128)(2,1)S(1)}, bf16[1280,2,64]{0,2,1:T(8,128)(2,1)}, u32[]{:S(2)}) copy-start(bf16[1280,2,64]{0,2,1:T(8,128)(2,1)} %copy-done.3) | copy-start | bytes 983044
  315.8 9.0 %copy-start.8 = (bf16[1280,2,64]{0,2,1:T(8,128)(2,1)S(1)}, bf16[1280,2,64]{0,2,1:T(8,128)(2,1)}, u32[]{:S(2)}) copy-start(bf16[1280,2,64]{0,2,1:T(8,128)(2,1)} %copy-done.7) | copy-start | bytes 983044
  315.8 10.3 %copy-start.25 = (bf16[1280,2,64]{0,2,1:T(8,128)(2,1)S(1)}, bf16[1280,2,64]{0,2,1:T(8,128)(2,1)}, u32[]{:S(2)}) copy-start(bf16[1280,2,64]{0,2,1:T(8,128)(2,1)} %copy-done.24) | copy-start | bytes 983044
  395.8 6.0 copy-start.17
  395.8 165.4 %all-to-all-start.1 = ((bf16[4,2,460800]{2,1,0:T(2,128)(2,1)}), bf16[4,2,460800]{2,1,0:T(2,128)(2,1)}, u32[]{:S(2)}, u32[]{:S(2)}) async-start(bf16[4,2,460800]{2,1,0:T(2,128)(2,1)} %reshape.125), calls=%async_computation.1 | async-start | bytes 14745600 | tf_op jit(solution)/shard_map/all_to_all | solution.py:92
  612.7 13.9 %copy-start.18 = (bf16[1280,2,64]{0,2,1:T(8,128)(2,1)S(1)}, bf16[1280,2,64]{0,2,1:T(8,128)(2,1)}, u32[]{:S(2)}) copy-start(bf16[1280,2,64]{0,2,1:T(8,128)(2,1)} %get-tuple-element.42) | copy-start | bytes 983044
  614.2 8.3 %copy-start.2 = (bf16[320,1280]{1,0:T(8,128)(2,1)S(1)}, bf16[320,1280]{1,0:T(8,128)(2,1)}, u32[]{:S(2)}) copy-start(bf16[320,1280]{1,0:T(8,128)(2,1)} %squeeze.92) | copy-start | bytes 2457604
  614.2 9.6 %copy-start.1 = (bf16[320,1280]{1,0:T(8,128)(2,1)S(1)}, bf16[320,1280]{1,0:T(8,128)(2,1)}, u32[]{:S(2)}) copy-start(bf16[320,1280]{1,0:T(8,128)(2,1)} %squeeze.93) | copy-start | bytes 2457604
Sparse Core Ops, SparseCore 0:
  294.9 35.7 reduce-scatter.8
  366.4 67.7 reduce-scatter.6
where the time goes:
time: 659 us; the launch traced here: 649 us
  local copies, waits for them, and re-layouts  243 us (37%)
  waiting for transfers between devices  160 us (24%)
  blocking collectives  154 us (23%)
  matrix products  37.1 us (6%)
  starting transfers between devices  29.3 us (4%)
  between operations  15 us (2%)
  other arithmetic  10.6 us (2%)
    unnamed x96, local copies, waits for them, and re-layouts  175 us
    all_gather x4, blocking collectives, circulate(): lax.all_gather(data, 'ch', axis=0, tiled=True)  154 us
    all_to_all x1, waiting for transfers between devices, on_device(): lax.all_to_all(jnp.transpose(spatial_weight, (0, 2, 1)), 'ch', split_axis...  153 us
    squeeze x10, local copies, waits for them, and re-layouts, contract(): weights[position]  21.6 us
    dot_general x20, matrix products, contract(): jnp.dot(weights[position], pieces[position], preferred_element_type=jnp.f...  19.3 us
    ppermute x8, starting transfers between devices, passed_along(): return lax.ppermute(shard, axis, pairs)  17 us
    slice x2, local copies, waits for them, and re-layouts, spatial_piece(): window = lax.slice_in_dim(padded, first_cell, first_cell + RT * W, axis=2)  13.8 us
  transfers between devices with their start and end apart: 12, of which 5 were waited for; matrix products, arithmetic and copies ran while one was open for 31% of the time, Pallas kernels for 0%

commit v1 on v0

--- a/solution.py
+++ b/solution.py
@@ -12,6 +12,22 @@
     ((row_step, col_step) for row_step in (-1, 0, 1) for col_step in (-1, 0, 1))
 )
 frame_offsets = (-1, 0, 1)
+
+
+def swapped_with_each(array, axis, split, join):
+    ways, here = (lax.axis_size(axis), lax.axis_index(axis))
+    width = array.shape[split] // ways
+    dims = list(array.shape)
+    dims[split] = width
+    height = dims[join]
+    dims[join] = height * ways
+    full = jnp.zeros(dims, array.dtype)
+    for mask in range(ways):
+        part = lax.dynamic_slice_in_dim(array, (here ^ mask) * width, width, axis=split)
+        if mask:
+            part = lax.ppermute(part, axis, [(d, d ^ mask) for d in range(ways)])
+        full = lax.dynamic_update_slice_in_dim(full, part, (here ^ mask) * height, axis=join)
+    return full
 
 
 def passed_along(shard, axis, by):
@@ -89,9 +105,7 @@
     channels, tile_cells = latents.shape
     grad_scale = 1.0 / math.sqrt(tile_cells * lax.axis_size("st"))
     spatial_back, temporal_back = (
-        lax.all_to_all(
-            jnp.transpose(spatial_weight, (0, 2, 1)), "ch", split_axis=1, concat_axis=2, tiled=True
-        ),
+        swapped_with_each(jnp.transpose(spatial_weight, (0, 2, 1)), "ch", 1, 2),
         lax.all_to_all(
             jnp.transpose(temporal_weight, (0, 2, 1)), "ch", split_axis=1, concat_axis=2, tiled=True
         ),

time: 659 us -> 602 us (0.914)
  the two profiles are of different devices: /device:TPU:0 before, /device:TPU:10 now
where the time goes in v1:
time: 602 us; the launch traced here: 593 us
  waiting for transfers between devices  188 us (31%)
  local copies, waits for them, and re-layouts  159 us (26%)
  blocking collectives  151 us (25%)
  starting transfers between devices  37.6 us (6%)
  matrix products  30.8 us (5%)
  between operations  15.3 us (3%)
  other arithmetic  10.6 us (2%)
    ppermute x3, waiting for transfers between devices, swapped_with_each(): part = lax.ppermute(part, axis, [(d, d ^ mask) for d in range(ways)])  180 us
    all_gather x4, blocking collectives, circulate(): lax.all_gather(data, 'ch', axis=0, tiled=True)  151 us
    unnamed x100, local copies, waits for them, and re-layouts  109 us
    ppermute x8, starting transfers between devices, passed_along(): return lax.ppermute(shard, axis, pairs)  28.7 us
    dot_general x12, matrix products, outer_sums(): lax.dot_general(gradient, tap_piece, contraction, preferred_element_type=...  14.6 us
    slice x2, local copies, waits for them, and re-layouts, spatial_piece(): window = lax.slice_in_dim(padded, first_cell, first_cell + RT * W, axis=2)  13.8 us
  transfers between devices with their start and end apart: 14, of which 7 were waited for; matrix products, arithmetic and copies ran while one was open for 18% of the time, Pallas kernels for 0%

profile of v1, /device:TPU:10, one launch (start us, length us, event | category | flops | bytes accessed | tf_op | source)
XLA Modules:
  0.0 592.6 jit_solution(7276243369798057651)
XLA Ops:
  7.2 7.7 %copy.22 = bf16[3,320,1280]{1,0,2:T(4,128)(2,1)} copy(bf16[3,320,1280]{2,1,0:T(8,128)(2,1)} %param.6) | data formatting | bytes 4915200 | tf_op args[2]
  14.9 5.3 all-to-all-start
  20.3 2.4 collective-permute-start.5
  26.1 3.6 collective-permute-start.1
  32.7 86.6 %all_gather.16 = bf16[1280,256]{1,0:T(8,128)(2,1)S(1)} all-gather(bf16[320,256]{1,0:T(8,128)(2,1)S(1)} %pad_maximum_fusion.2), channel_id=1, replica_groups=mesh['groups'=2,'st'=4,'ch'=4] {'ch'}, dimensions={0}, use_global_device_ids=true | all-gather | bytes 819200 | tf_op jit(solution)/shard_map/all_gather | solution.py:44
  119.3 21.6 %all_gather.14 = bf16[1280,2,130]{2,1,0:T(2,128)(2,1)S(1)} all-gather(bf16[320,2,130]{2,1,0:T(2,128)(2,1)S(1)} %copy.12), channel_id=1, replica_groups=mesh['groups'=2,'st'=4,'ch'=4] {'ch'}, dimensions={0}, use_global_device_ids=true | all-gather | bytes 832000 | tf_op jit(solution)/shard_map/all_gather | solution.py:44
  140.9 4.9 copy.58
  145.8 2.3 fusion.83
  148.1 2.8 squeeze.85
  150.9 2.8 squeeze.84
  160.1 12.7 %collective-permute-start.9 = (bf16[320,2,32]{0,2,1:T(8,128)(2,1)S(1)}, bf16[320,2,32]{0,2,1:T(8,128)(2,1)S(1)}, u32[]{:S(2)}, u32[]{:S(2)}) collective-permute-start(bf16[320,2,32]{0,2,1:T(8,128)(2,1)S(1)} %get-tuple-element.29), channel_id=1, source_target_pairs={{0,4},{4,8},{8,12},{1,5},{5,9},{9,13},{2,6},{6,10},{10,14},{3,7},{... | collective-permute-start | bytes 122888 | tf_op jit(solution)/shard_map/ppermute | solution.py:36
  172.8 6.9 %fusion.85 = (bf16[1280,2,64]{2,1,0:T(2,128)(2,1)S(1)}, bf16[1280,2,64]{2,1,0:T(2,128)(2,1)}, bf16[1280,2,64]{2,1,0:T(2,128)(2,1)}, bf16[1280,2,64]{2,1,0:T(2,12...) fusion(bf16[1280,2,130]{2,1,0:T(2,128)(2,1)S(1)} %all_gather.14), kind=kLoop, calls=%fused_computation.158 | loop fusion | bytes 5898240 | tf_op jit(solution)/shard_map/slice | solution.py:65
  179.7 2.0 copy.42
  183.8 2.0 copy.39
  185.8 2.0 copy.43
  189.8 2.0 copy.40
  191.9 2.0 copy.44
  196.1 3.6 collective-permute-start.10
  202.5 24.3 %all_gather.17 = bf16[1280,2,130]{2,1,0:T(2,128)(2,1)S(1)} all-gather(bf16[320,2,130]{2,1,0:T(2,128)(2,1)S(1)} %copy.25), channel_id=1, replica_groups=mesh['groups'=2,'st'=4,'ch'=4] {'ch'}, dimensions={0}, use_global_device_ids=true | all-gather | bytes 832000 | tf_op jit(solution)/shard_map/all_gather | solution.py:44
  226.8 6.9 %fusion.84 = (bf16[1280,2,64]{2,1,0:T(2,128)(2,1)}, bf16[1280,2,64]{2,1,0:T(2,128)(2,1)}, bf16[1280,2,64]{2,1,0:T(2,128)(2,1)}, bf16[1280,2,64]{2,1,0:T(2,128)(2...) fusion(bf16[1280,2,130]{2,1,0:T(2,128)(2,1)S(1)} %all_gather.17), kind=kLoop, calls=%fused_computation.157 | loop fusion | bytes 5898240 | tf_op jit(solution)/shard_map/slice | solution.py:65
  237.0 2.2 copy.49
  239.2 2.0 copy.52
  241.2 2.0 copy.55
  245.3 2.0 copy.51
  247.3 2.0 copy.54
  249.4 2.7 broadcast_select_fusion.14
  254.0 2.5 broadcast_select_fusion.8
  264.7 4.3 collective-permute-done.2
  269.1 18.3 %all_gather.15 = bf16[1280,256]{1,0:T(8,128)(2,1)S(1)} all-gather(bf16[320,256]{1,0:T(8,128)(2,1)S(1)} %pad_maximum_fusion.1), channel_id=1, replica_groups=mesh['groups'=2,'st'=4,'ch'=4] {'ch'}, dimensions={0}, use_global_device_ids=true | all-gather | bytes 819200 | tf_op jit(solution)/shard_map/all_gather | solution.py:44
  289.0 6.0 %copy.37 = bf16[3,320,1280]{1,0,2:T(4,128)(2,1)} copy(bf16[3,320,1280]{2,1,0:T(8,128)(2,1)S(1)} %pad_maximum_fusion) | data formatting | bytes 4915200
  295.0 8.4 %reshape.105 = bf16[1280,960]{1,0:T(8,128)(2,1)} reshape(bf16[1280,3,320]{2,1,0:T(4,128)(2,1)} %bitcast.212) | data formatting | bytes 4915200
  303.5 2.2 fusion.1
  314.6 2.3 fusion.17
  316.9 20.2 %copy.35 = bf16[9,320,1280]{1,0,2:T(8,128)(2,1)} copy(bf16[9,320,1280]{2,1,0:T(8,128)(2,1)} %fusion.17) | data formatting | bytes 14745600
  337.1 18.7 %reshape.103 = bf16[1280,2880]{1,0:T(8,128)(2,1)} reshape(bf16[1280,9,320]{2,1,0:T(8,128)(2,1)} %bitcast.208) | data formatting | bytes 14745600
  355.9 9.5 %dynamic-slice_bitcast_fusion = (bf16[9,320,320]{1,2,0:T(8,128)(2,1)S(1)}, bf16[9,320,320]{1,2,0:T(8,128)(2,1)}, bf16[9,320,320]{1,2,0:T(8,128)(2,1)}) fusion(bf16[9,320,1280]{2,1,0:T(8,128)(2,1)} %param.5, s32[]{:T(128)S(6)} %select_n.221, s32[]{:T(128)S(6)} %select_n.219, s32[]{:T(128)S(6)} %select_n.220), kind=kLoop, calls=%fused_computation.37 | loop fusion | bytes 11059212 | tf_op jit(solution)/shard_map/dynamic_slice | solution.py:26
  365.4 2.1 collective-permute-start.6
  369.9 3.3 bitcast_dynamic-update-slice_fusion
  373.2 86.4 %collective-permute-done.6 = bf16[9,320,320]{1,2,0:T(8,128)(2,1)} collective-permute-done((bf16[9,320,320]{1,2,0:T(8,128)(2,1)}, bf16[9,320,320]{1,2,0:T(8,128)(2,1)}, u32[]{:S(2)}, u32[]{:S(2)}) %collective-permute-start.6) | collective-permute-done | bytes 1843232 | tf_op jit(solution)/shard_map/ppermute | solution.py:28
  459.5 2.1 constant_dynamic-update-slice_fusion.1
  461.6 50.2 %collective-permute-done.7 = bf16[9,320,320]{1,2,0:T(8,128)(2,1)} collective-permute-done((bf16[9,320,320]{1,2,0:T(8,128)(2,1)}, bf16[9,320,320]{1,2,0:T(8,128)(2,1)}, u32[]{:S(2)}, u32[]{:S(2)}) %collective-permute-start.7) | collective-permute-done | bytes 1843232 | tf_op jit(solution)/shard_map/ppermute | solution.py:28
  511.8 2.1 constant_dynamic-update-slice_fusion
  513.9 43.4 %collective-permute-done.8 = bf16[9,320,320]{1,2,0:T(8,128)(2,1)} collective-permute-done((bf16[9,320,320]{1,2,0:T(8,128)(2,1)S(1)}, bf16[9,320,320]{1,2,0:T(8,128)(2,1)}, u32[]{:S(2)}, u32[]{:S(2)}) %collective-permute-start.8) | collective-permute-done | bytes 1843232 | tf_op jit(solution)/shard_map/ppermute | solution.py:28
  557.3 2.1 constant_dynamic-update-slice_fusion.2
  566.2 2.7 reshape.106
  571.3 5.6 reshape.104
  576.9 6.0 %copy.36 = bf16[9,320,320]{2,1,0:T(8,128)(2,1)S(1)} copy(bf16[9,320,320]{1,0,2:T(8,128)(2,1)} %bitcast.213) | data formatting | bytes 3686400
  582.9 2.5 convert_multiply_fusion
  (160 shorter events, 59.1 us)
Async XLA Ops:
  7.2 13.0 %copy-start = (bf16[320,128]{1,0:T(8,128)(2,1)S(1)}, bf16[320,128]{1,0:T(8,128)(2,1)}, u32[]{:S(2)}) copy-start(bf16[320,128]{1,0:T(8,128)(2,1)} %param.7) | copy-start | bytes 245764
  7.2 16.9 %copy-start.33 = (bf16[320,128]{1,0:T(8,128)(2,1)S(1)}, bf16[320,128]{1,0:T(8,128)(2,1)}, u32[]{:S(2)}) copy-start(bf16[320,128]{1,0:T(8,128)(2,1)} %param.4) | copy-start | bytes 245764
  14.9 126.1 %all-to-all-start = ((bf16[3,1280,320]{2,0,1:T(4,128)(2,1)}), bf16[3,1280,320]{2,0,1:T(4,128)(2,1)}, u32[]{:S(2)}, u32[]{:S(2)}) async-start(bf16[3,1280,320]{2,0,1:T(4,128)(2,1)} %bitcast.211), calls=%async_computation | async-start | bytes 7864320 | tf_op jit(solution)/shard_map/all_to_all | solution.py:109
  20.2 546.0 %reduce-scatter.9.cloned.1.call-start = ((), (), s32[]{:S(2)}) async-start(), calls=%async_computation.4 | async-start | bytes 3276800
  20.3 12.3 %collective-permute-start.5 = (bf16[320,64]{1,0:T(8,128)(2,1)S(1)}, bf16[320,64]{1,0:T(8,128)(2,1)S(1)}, u32[]{:S(2)}, u32[]{:S(2)}) collective-permute-start(bf16[320,64]{1,0:T(8,128)(2,1)S(1)} %get-tuple-element.33), channel_id=1, source_target_pairs={{8,0},{12,4},{9,1},{13,5},{10,2},{14,6},{11,3},{15,7},{24,16},{28,... | collective-permute-start | bytes 122888 | tf_op jit(solution)/shard_map/ppermute | solution.py:36
  22.7 9.8 %collective-permute-start.4 = (bf16[320,64]{1,0:T(8,128)(2,1)S(1)}, bf16[320,64]{1,0:T(8,128)(2,1)S(1)}, u32[]{:S(2)}, u32[]{:S(2)}) collective-permute-start(bf16[320,64]{1,0:T(8,128)(2,1)S(1)} %get-tuple-element.32), channel_id=1, source_target_pairs={{0,8},{4,12},{1,9},{5,13},{2,10},{6,14},{3,11},{7,15},{16,24},{20,... | collective-permute-start | bytes 122888 | tf_op jit(solution)/shard_map/ppermute | solution.py:36
  24.2 5.6 collective-permute-start
  26.1 5.4 collective-permute-start.1
  160.1 39.6 %collective-permute-start.9 = (bf16[320,2,32]{0,2,1:T(8,128)(2,1)S(1)}, bf16[320,2,32]{0,2,1:T(8,128)(2,1)S(1)}, u32[]{:S(2)}, u32[]{:S(2)}) collective-permute-start(bf16[320,2,32]{0,2,1:T(8,128)(2,1)S(1)} %get-tuple-element.29), channel_id=1, source_target_pairs={{0,4},{4,8},{8,12},{1,5},{5,9},{9,13},{2,6},{6,10},{10,14},{3,7},{... | collective-permute-start | bytes 122888 | tf_op jit(solution)/shard_map/ppermute | solution.py:36
  196.1 5.4 collective-permute-start.10
  237.0 19.6 %slice-start = ((s8[7372800]{0:T(1024)(128)(4,1)}), s8[3178496]{0:T(1024)(128)(4,1)S(1)}, s32[]{:S(2)}) async-start(s8[7372800]{0:T(1024)(128)(4,1)} %bitcast.209), calls=%async_computation.5 | async-start | bytes 6356992
  249.4 7.2 %slice-start.1 = ((s8[7372800]{0:T(1024)(128)(4,1)}), s8[4194304]{0:T(1024)(128)(4,1)S(1)}, s32[]{:S(2)}) async-start(s8[7372800]{0:T(1024)(128)(4,1)} %bitcast.209), calls=%async_computation.6 | async-start | bytes 8388608
  249.4 7.6 %copy-start.17 = (bf16[1280,2,64]{0,2,1:T(8,128)(2,1)S(1)}, bf16[1280,2,64]{0,2,1:T(8,128)(2,1)}, u32[]{:S(2)}) copy-start(bf16[1280,2,64]{0,2,1:T(8,128)(2,1)} %copy.44) | copy-start | bytes 983044
  249.4 7.6 %copy-start.18 = (bf16[1280,2,64]{0,2,1:T(8,128)(2,1)S(1)}, bf16[1280,2,64]{0,2,1:T(8,128)(2,1)}, u32[]{:S(2)}) copy-start(bf16[1280,2,64]{0,2,1:T(8,128)(2,1)} %copy.47) | copy-start | bytes 983044
  249.4 7.6 %copy-start.19 = (bf16[1280,2,64]{0,2,1:T(8,128)(2,1)S(1)}, bf16[1280,2,64]{0,2,1:T(8,128)(2,1)}, u32[]{:S(2)}) copy-start(bf16[1280,2,64]{0,2,1:T(8,128)(2,1)} %copy.41) | copy-start | bytes 983044
  249.4 7.6 %copy-start.21 = (bf16[1280,2,64]{0,2,1:T(8,128)(2,1)S(1)}, bf16[1280,2,64]{0,2,1:T(8,128)(2,1)}, u32[]{:S(2)}) copy-start(bf16[1280,2,64]{0,2,1:T(8,128)(2,1)} %copy.48) | copy-start | bytes 983044
  249.4 7.6 %copy-start.22 = (bf16[1280,2,64]{0,2,1:T(8,128)(2,1)S(1)}, bf16[1280,2,64]{0,2,1:T(8,128)(2,1)}, u32[]{:S(2)}) copy-start(bf16[1280,2,64]{0,2,1:T(8,128)(2,1)} %copy.51) | copy-start | bytes 983044
  249.4 7.6 %copy-start.23 = (bf16[1280,2,64]{0,2,1:T(8,128)(2,1)S(1)}, bf16[1280,2,64]{0,2,1:T(8,128)(2,1)}, u32[]{:S(2)}) copy-start(bf16[1280,2,64]{0,2,1:T(8,128)(2,1)} %copy.54) | copy-start | bytes 983044
  252.1 7.1 %copy-start.3 = (bf16[1280,2,64]{0,2,1:T(8,128)(2,1)}, bf16[1280,2,64]{0,2,1:T(8,128)(2,1)S(1)}, u32[]{:S(2)}) copy-start(bf16[1280,2,64]{0,2,1:T(8,128)(2,1)S(1)} %get-tuple-element.49) | copy-start | bytes 983044
  252.1 7.5 %copy-start.1 = (bf16[1280,2,64]{0,2,1:T(8,128)(2,1)}, bf16[1280,2,64]{0,2,1:T(8,128)(2,1)S(1)}, u32[]{:S(2)}) copy-start(bf16[1280,2,64]{0,2,1:T(8,128)(2,1)S(1)} %get-tuple-element.50) | copy-start | bytes 983044
  256.6 4.2 copy-start.5
  256.6 4.2 copy-start.7
  256.6 4.3 copy-start.9
  258.1 30.2 %copy-start.11 = (bf16[1280,2,64]{0,2,1:T(8,128)(2,1)}, bf16[1280,2,64]{0,2,1:T(8,128)(2,1)S(1)}, u32[]{:S(2)}) copy-start(bf16[1280,2,64]{0,2,1:T(8,128)(2,1)S(1)} %get-tuple-element.37) | copy-start | bytes 983044
  258.1 30.2 %copy-start.13 = (bf16[1280,2,64]{0,2,1:T(8,128)(2,1)}, bf16[1280,2,64]{0,2,1:T(8,128)(2,1)S(1)}, u32[]{:S(2)}) copy-start(bf16[1280,2,64]{0,2,1:T(8,128)(2,1)S(1)} %get-tuple-element.41) | copy-start | bytes 983044
  258.1 30.2 %copy-start.20 = (bf16[1280,2,64]{0,2,1:T(8,128)(2,1)}, bf16[1280,2,64]{0,2,1:T(8,128)(2,1)S(1)}, u32[]{:S(2)}) copy-start(bf16[1280,2,64]{0,2,1:T(8,128)(2,1)S(1)} %get-tuple-element.38) | copy-start | bytes 983044
  260.9 3.8 collective-permute-start.3
  262.7 6.3 %collective-permute-start.2 = (bf16[320,64]{1,0:T(8,128)(2,1)S(1)}, bf16[320,64]{1,0:T(8,128)(2,1)S(1)}, u32[]{:S(2)}, u32[]{:S(2)}) collective-permute-start(bf16[320,64]{1,0:T(8,128)(2,1)S(1)} %get-tuple-element.34), channel_id=1, source_target_pairs={{0,8},{4,12},{1,9},{5,13},{2,10},{6,14},{3,11},{7,15},{16,24},{20,... | collective-permute-start | bytes 122888 | tf_op jit(solution)/shard_map/ppermute | solution.py:36
  295.0 10.8 %copy-start.10 = (bf16[1280,2,64]{0,2,1:T(8,128)(2,1)S(1)}, bf16[1280,2,64]{0,2,1:T(8,128)(2,1)}, u32[]{:S(2)}) copy-start(bf16[1280,2,64]{0,2,1:T(8,128)(2,1)} %copy-done.9) | copy-start | bytes 983044
  295.0 12.0 %copy-start.14 = (bf16[1280,2,64]{0,2,1:T(8,128)(2,1)S(1)}, bf16[1280,2,64]{0,2,1:T(8,128)(2,1)}, u32[]{:S(2)}) copy-start(bf16[1280,2,64]{0,2,1:T(8,128)(2,1)} %copy-done.13) | copy-start | bytes 983044
  295.0 13.3 %copy-start.4 = (bf16[1280,2,64]{0,2,1:T(8,128)(2,1)S(1)}, bf16[1280,2,64]{0,2,1:T(8,128)(2,1)}, u32[]{:S(2)}) copy-start(bf16[1280,2,64]{0,2,1:T(8,128)(2,1)} %copy-done.3) | copy-start | bytes 983044
  295.0 14.6 %copy-start.8 = (bf16[1280,2,64]{0,2,1:T(8,128)(2,1)S(1)}, bf16[1280,2,64]{0,2,1:T(8,128)(2,1)}, u32[]{:S(2)}) copy-start(bf16[1280,2,64]{0,2,1:T(8,128)(2,1)} %copy-done.7) | copy-start | bytes 983044
  295.0 15.8 %copy-start.12 = (bf16[1280,2,64]{0,2,1:T(8,128)(2,1)S(1)}, bf16[1280,2,64]{0,2,1:T(8,128)(2,1)}, u32[]{:S(2)}) copy-start(bf16[1280,2,64]{0,2,1:T(8,128)(2,1)} %copy-done.11) | copy-start | bytes 983044
  295.0 17.1 %copy-start.2 = (bf16[1280,2,64]{0,2,1:T(8,128)(2,1)S(1)}, bf16[1280,2,64]{0,2,1:T(8,128)(2,1)}, u32[]{:S(2)}) copy-start(bf16[1280,2,64]{0,2,1:T(8,128)(2,1)} %copy-done.1) | copy-start | bytes 983044
  295.0 18.3 %copy-start.6 = (bf16[1280,2,64]{0,2,1:T(8,128)(2,1)S(1)}, bf16[1280,2,64]{0,2,1:T(8,128)(2,1)}, u32[]{:S(2)}) copy-start(bf16[1280,2,64]{0,2,1:T(8,128)(2,1)} %copy-done.5) | copy-start | bytes 983044
  303.5 267.8 %reduce-scatter.7.cloned.1.call-start = ((), (), s32[]{:S(2)}) async-start(), calls=%async_computation.3 | async-start | bytes 9420800
  365.4 94.1 %collective-permute-start.6 = (bf16[9,320,320]{1,2,0:T(8,128)(2,1)}, bf16[9,320,320]{1,2,0:T(8,128)(2,1)}, u32[]{:S(2)}, u32[]{:S(2)}) collective-permute-start(bf16[9,320,320]{1,2,0:T(8,128)(2,1)} %get-tuple-element.5), channel_id=1, source_target_pairs={{0,1},{1,0},{2,3},{3,2},{4,5},{5,4},{6,7},{7,6},{8,9},{9,8},{10,11... | collective-permute-start | bytes 5529608 | tf_op jit(solution)/shard_map/ppermute | solution.py:28
  367.5 144.3 %collective-permute-start.7 = (bf16[9,320,320]{1,2,0:T(8,128)(2,1)}, bf16[9,320,320]{1,2,0:T(8,128)(2,1)}, u32[]{:S(2)}, u32[]{:S(2)}) collective-permute-start(bf16[9,320,320]{1,2,0:T(8,128)(2,1)} %get-tuple-element.6), channel_id=1, source_target_pairs={{0,2},{1,3},{2,0},{3,1},{4,6},{5,7},{6,4},{7,5},{8,10},{9,11},{10,... | collective-permute-start | bytes 5529608 | tf_op jit(solution)/shard_map/ppermute | solution.py:28
  368.1 189.1 %collective-permute-start.8 = (bf16[9,320,320]{1,2,0:T(8,128)(2,1)S(1)}, bf16[9,320,320]{1,2,0:T(8,128)(2,1)}, u32[]{:S(2)}, u32[]{:S(2)}) collective-permute-start(bf16[9,320,320]{1,2,0:T(8,128)(2,1)S(1)} %get-tuple-element.4), channel_id=1, source_target_pairs={{0,3},{1,2},{2,1},{3,0},{4,7},{5,6},{6,5},{7,4},{8,11},{9,10},{10,... | collective-permute-start | bytes 5529608 | tf_op jit(solution)/shard_map/ppermute | solution.py:28
  373.1 186.2 %copy-start.27 = (bf16[1280,2,64]{0,2,1:T(8,128)(2,1)S(1)}, bf16[1280,2,64]{0,2,1:T(8,128)(2,1)}, u32[]{:S(2)}) copy-start(bf16[1280,2,64]{0,2,1:T(8,128)(2,1)} %get-tuple-element.52) | copy-start | bytes 983044
  373.1 186.7 %copy-start.30 = (bf16[1280,2,64]{0,2,1:T(8,128)(2,1)S(1)}, bf16[1280,2,64]{0,2,1:T(8,128)(2,1)}, u32[]{:S(2)}) copy-start(bf16[1280,2,64]{0,2,1:T(8,128)(2,1)} %get-tuple-element.46) | copy-start | bytes 983044
  373.2 187.2 %copy-start.32 = (bf16[1280,2,64]{0,2,1:T(8,128)(2,1)S(1)}, bf16[1280,2,64]{0,2,1:T(8,128)(2,1)}, u32[]{:S(2)}) copy-start(bf16[1280,2,64]{0,2,1:T(8,128)(2,1)} %get-tuple-element.40) | copy-start | bytes 983044
  461.6 99.2 %copy-start.26 = (bf16[1280,2,64]{0,2,1:T(8,128)(2,1)S(1)}, bf16[1280,2,64]{0,2,1:T(8,128)(2,1)}, u32[]{:S(2)}) copy-start(bf16[1280,2,64]{0,2,1:T(8,128)(2,1)} %get-tuple-element.51) | copy-start | bytes 983044
  461.6 99.7 %copy-start.29 = (bf16[1280,2,64]{0,2,1:T(8,128)(2,1)S(1)}, bf16[1280,2,64]{0,2,1:T(8,128)(2,1)}, u32[]{:S(2)}) copy-start(bf16[1280,2,64]{0,2,1:T(8,128)(2,1)} %get-tuple-element.45) | copy-start | bytes 983044
  513.9 47.9 %copy-start.31 = (bf16[1280,2,64]{0,2,1:T(8,128)(2,1)S(1)}, bf16[1280,2,64]{0,2,1:T(8,128)(2,1)}, u32[]{:S(2)}) copy-start(bf16[1280,2,64]{0,2,1:T(8,128)(2,1)} %get-tuple-element.39) | copy-start | bytes 983044
  513.9 48.3 %copy-start.25 = (bf16[1280,2,64]{0,2,1:T(8,128)(2,1)S(1)}, bf16[1280,2,64]{0,2,1:T(8,128)(2,1)}, u32[]{:S(2)}) copy-start(bf16[1280,2,64]{0,2,1:T(8,128)(2,1)} %get-tuple-element.48) | copy-start | bytes 983044
  513.9 48.8 %copy-start.28 = (bf16[1280,2,64]{0,2,1:T(8,128)(2,1)S(1)}, bf16[1280,2,64]{0,2,1:T(8,128)(2,1)}, u32[]{:S(2)}) copy-start(bf16[1280,2,64]{0,2,1:T(8,128)(2,1)} %get-tuple-element.42) | copy-start | bytes 983044
  559.8 4.4 copy-start.15
  (2 other events, 5.7 us)
Sparse Core Ops, SparseCore 0:
  303.6 34.9 reduce-scatter.8
  356.0 66.9 reduce-scatter.6
